TPU v7x, 32 devices: a whole 2x2x4 slice. The times are simulated.
32 devices in a mesh: dp: 2 (over y), expert: 16 (over z, x, core).
Axes of the slice: x: 2, y: 2, z: 4, core: 2. Of those that a mesh axis runs over, the one named last changes fastest.
Arguments:
- tokens: bfloat16 [512, 2880], P(('dp', 'expert')), may hold values from -6 to 6
- grad_out: bfloat16 [512, 2880], P(('dp', 'expert')), may hold values from -6 to 6
- route_ids: int32 [512, 4], P(('dp', 'expert')), may hold values from 0 to 4, all different within a row; in each aligned block of 16 rows (0 to 15, 16 to 31, ...) at most 16 rows name the same one
- route_prob: float32 [512, 4], P(('dp', 'expert')), may hold values from 0.05 to 1
- device_expert: int32 [16], replicated, may hold values from 0 to 4, as said below
- unit_count: int32 [16], replicated, may hold values from 264 to 480, as said below
- expert_weights: bfloat16 [16, 480, 8640], P('expert'), may hold values from -0.109375 to 0.109375
Outputs:
- grad_tokens: bfloat16 [512, 2880], P(('dp', 'expert'))
- grad_weights: bfloat16 [16, 480, 8640], P('expert', 'dp')
Inputs may be any that keep to these rules, and one draw needn't show every extreme that they name: `route_ids`: each row names 4 different experts; the 16 rows of one device name each expert at most 16 times, and in every draw some device names some expert exactly 16 times. `device_expert`: aligned blocks of 16 indices of expert hold 5 experts, ids rising by one from 5 times the block's number; the indices of one expert are consecutive, 3 or 4 of them; every expert has a group. `unit_count`: the counts of the indices of one expert sum to 1440; rows of expert_weights at or past a slot's count are not part of the model.
All inputs are finite; a program needn't handle non-finite values.
Results may differ from a plain program's by a relative error of at most 0.0058.
Values may be sent and summed in bfloat16 or wider, within the bound.
A program may use at most 128 MiB of HBM per device.

v0:
```python
import jax
import jax.numpy as jnp
from jax import lax
from jax.sharding import PartitionSpec as P


def silu_parts(preact):
    sigma = jax.nn.sigmoid(preact)
    return (preact * sigma, sigma * (1.0 + preact * (1.0 - sigma)))


def unit_work(token_rows, grad_rows, slot_weights, unit_mask):
    width = token_rows.shape[1]
    gate_rows = slot_weights[:, :width]
    up_rows = slot_weights[:, width : 2 * width]
    down_rows = slot_weights[:, 2 * width :]
    contract = (((1,), (1,)), ((), ()))
    gate_pre = lax.dot_general(token_rows, gate_rows, contract, preferred_element_type=jnp.float32)
    up_pre = lax.dot_general(token_rows, up_rows, contract, preferred_element_type=jnp.float32)
    back_grad = lax.dot_general(grad_rows, down_rows, contract, preferred_element_type=jnp.float32)
    active, slope = silu_parts(gate_pre)
    hidden = (active * up_pre * unit_mask).astype(jnp.bfloat16)
    grad_gate = (back_grad * up_pre * slope * unit_mask).astype(jnp.bfloat16)
    grad_up = (back_grad * active * unit_mask).astype(jnp.bfloat16)
    partial_value = jnp.dot(grad_gate, gate_rows, preferred_element_type=jnp.float32) + jnp.dot(
        grad_up, up_rows, preferred_element_type=jnp.float32
    )
    return (partial_value, hidden, grad_gate, grad_up)


def weight_terms(token_rows, grad_rows, hidden, grad_gate, grad_up):
    rows_first = (((0,), (0,)), ((), ()))
    return jnp.concatenate(
        [
            lax.dot_general(grad_gate, token_rows, rows_first, preferred_element_type=jnp.float32),
            lax.dot_general(grad_up, token_rows, rows_first, preferred_element_type=jnp.float32),
            lax.dot_general(hidden, grad_rows, rows_first, preferred_element_type=jnp.float32),
        ],
        axis=1,
    )


def send_back(partial_value):
    return lax.all_to_all(partial_value, "expert", split_axis=0, concat_axis=0, tiled=True)


def shards(tokens, grad_out, route_ids, route_prob, device_expert, unit_count, expert_weights):
    token_count, width = tokens.shape
    top_count = route_ids.shape[1]
    devices = lax.axis_size("expert")
    experts = 5 * devices // 16
    capacity = token_count * top_count * 4 // devices
    flat_ids = route_ids.reshape(-1)
    onehot = (flat_ids[:, None] == jnp.arange(experts, dtype=jnp.int32)[None, :]).astype(jnp.int32)
    rank_of = jnp.sum(onehot * jnp.cumsum(onehot, axis=0), axis=1) - 1
    picked = (flat_ids[None, None, :] == device_expert[:, None, None]) & (
        rank_of[None, None, :] == jnp.arange(capacity, dtype=jnp.int32)[None, :, None]
    )
    picked = picked.astype(jnp.float32).reshape(devices * capacity, token_count * top_count)
    by_token = picked.reshape(devices * capacity, token_count, top_count).sum(axis=2)
    route_scale = jnp.dot(picked, route_prob.reshape(-1), precision=lax.Precision.HIGHEST)
    by_token_low = by_token.astype(jnp.bfloat16)
    sent_rows = jnp.dot(by_token_low, tokens, preferred_element_type=jnp.float32).astype(
        jnp.bfloat16
    )
    sent_grads = (
        route_scale[:, None] * jnp.dot(by_token_low, grad_out, preferred_element_type=jnp.float32)
    ).astype(jnp.bfloat16)
    outgoing = jnp.stack([sent_rows, sent_grads], axis=1).reshape(devices, capacity, 2, width)
    position = lax.axis_index("expert")
    unit_limit = lax.dynamic_index_in_dim(unit_count, position, keepdims=False)
    slot_weights = expert_weights[0]
    slot_units = slot_weights.shape[0]
    unit_mask = (jnp.arange(slot_units, dtype=jnp.int32) < unit_limit).astype(jnp.float32)
    arrived = lax.all_to_all(outgoing, "expert", split_axis=0, concat_axis=0, tiled=True)
    row_pairs = arrived.reshape(-1, 2, width)
    partial_value, hidden, grad_gate, grad_up = unit_work(
        row_pairs[:, 0], row_pairs[:, 1], slot_weights, unit_mask
    )
    leading = (arrived.shape[0], arrived.shape[1])
    returned, all_rows, hidden, grad_gate, grad_up = (
        send_back(partial_value.reshape(leading + (width,))),
        arrived,
        hidden.reshape(leading + (slot_units,)),
        grad_gate.reshape(leading + (slot_units,)),
        grad_up.reshape(leading + (slot_units,)),
    )
    row_pairs = all_rows.reshape(-1, 2, width)
    token_rows = row_pairs[:, 0]
    grad_rows = row_pairs[:, 1]
    hidden = hidden.reshape(-1, slot_units)
    grad_gate = grad_gate.reshape(-1, slot_units)
    grad_up = grad_up.reshape(-1, slot_units)
    term_block = weight_terms(token_rows, grad_rows, hidden, grad_gate, grad_up)
    grad_weights = lax.psum_scatter(term_block, "dp", scatter_dimension=0, tiled=True)
    parts = returned.reshape(devices * capacity, width)
    grad_tokens = lax.dot_general(
        by_token,
        parts,
        (((0,), (0,)), ((), ())),
        precision=lax.Precision.HIGHEST,
        preferred_element_type=jnp.float32,
    )
    return (grad_tokens.astype(jnp.bfloat16), grad_weights.astype(jnp.bfloat16)[None])


def solution(mesh):
    in_specs = (
        P(("dp", "expert"), None),
        P(("dp", "expert"), None),
        P(("dp", "expert"), None),
        P(("dp", "expert"), None),
        P(),
        P(),
        P("expert", None, None),
    )
    out_specs = (P(("dp", "expert"), None), P("expert", "dp", None))
    return jax.shard_map(shards, mesh=mesh, in_specs=in_specs, out_specs=out_specs, check_vma=False)
```

profile of v0, /device:TPU:0, one launch (start us, length us, event | category | flops | bytes accessed | tf_op | source)
XLA Modules:
  0.0 333.3 jit_solution(180509648649561683)
XLA Ops:
  7.2 0.0 copy-start
  7.2 0.8 copy.22
  8.0 0.1 eq.51
  8.1 0.8 copy.25
  8.8 0.1 reshape.110
  8.9 0.1 fusion.16
  9.0 0.1 reduce_window_sum.11
  9.1 0.2 select_reduce_fusion
  9.3 0.7 iota_compare_fusion.1
  10.0 0.0 copy-start.2
  10.1 0.3 copy.23
  10.3 0.3 reshape.109
  10.6 0.1 fusion.22
  10.7 0.1 reduce_sum.19
  10.8 0.0 copy-done
  10.8 0.6 fusion
  11.4 1.0 copy.26
  12.4 0.0 copy-done.2
  12.4 1.7 convolution_convert_fusion
  14.2 1.8 copy.24
  16.0 0.3 pad_maximum_fusion
  16.3 1.8 copy.27
  18.1 0.0 copy-start.3
  18.1 7.5 %all-to-all-start = ((bf16[16,16,2,2880]{3,1,2,0:T(8,128)(2,1)}), bf16[16,16,2,2880]{3,1,2,0:T(8,128)(2,1)S(1)}, u32[]{:S(2)}, u32[]{:S(2)}) async-start(bf16[16,16,2,2880]{3,1,2,0:T(8,128)(2,1)} %copy.27), calls=%async_computation | async-start | bytes 6029312 | tf_op jit(solution)/shard_map/all_to_all | solution.py:75
  25.7 0.2 reduce-scatter.2.cloned.1.call-start
  25.9 0.0 copy-done.3
  25.9 0.6 dynamic_slice.4
  26.5 0.6 fusion.19
  27.2 55.5 %all-to-all-done = bf16[16,16,2,2880]{3,1,2,0:T(8,128)(2,1)S(1)} async-done(((bf16[16,16,2,2880]{3,1,2,0:T(8,128)(2,1)}), bf16[16,16,2,2880]{3,1,2,0:T(8,128)(2,1)S(1)}, u32[]{:S(2)}, u32[]{:S(2)}) %all-to-all-start) | async-done | bytes 2949152 | tf_op jit(solution)/shard_map/all_to_all | solution.py:75
  82.6 0.2 copy.28
  82.8 2.8 fusion.5
  85.6 3.2 fusion.8
  88.8 2.8 multiply_convert_fusion.1
  91.6 3.4 %fusion.10 = f32[480,2880]{1,0:T(8,128)} fusion(bf16[256,2,2880]{2,0,1:T(8,128)(2,1)S(1)} %bitcast.38, f32[256,480]{0,1:T(8,128)S(1)} %fusion.8, f32[480]{0:T(512)S(1)} %fusion.19, f32[256,480]{0,1:T(8,128)S(1)} %fusion.5), kind=kOutput, calls=%fused_computation.18 | convolution fusion | flops 708648960 | bytes 8022016 | tf_op jit(solution)/shard_map/dot_general | solution.py:37
  95.0 3.4 %fusion.11 = f32[480,2880]{1,0:T(8,128)} fusion(bf16[256,480]{0,1:T(8,128)(2,1)S(1)} %get-tuple-element.2, bf16[256,2,2880]{2,0,1:T(8,128)(2,1)S(1)} %bitcast.39), kind=kOutput, calls=%fused_computation.19 | convolution fusion | flops 707788800 | bytes 7282688 | tf_op jit(solution)/shard_map/dot_general | solution.py:36
  98.5 3.4 %fusion.12 = f32[480,2880]{1,0:T(8,128)} fusion(bf16[256,480]{0,1:T(8,128)(2,1)S(1)} %get-tuple-element.3, bf16[256,2,2880]{2,0,1:T(8,128)(2,1)S(1)} %bitcast.40), kind=kOutput, calls=%fused_computation.20 | convolution fusion | flops 707788800 | bytes 7282688 | tf_op jit(solution)/shard_map/dot_general | solution.py:35
  101.8 19.9 %concatenate.4 = f32[480,8640]{1,0:T(8,128)} concatenate(f32[480,2880]{1,0:T(8,128)} %fusion.12, f32[480,2880]{1,0:T(8,128)} %fusion.11, f32[480,2880]{1,0:T(8,128)} %fusion.10), dimensions={1} | concatenate | bytes 33177600 | tf_op jit(solution)/shard_map/concatenate | solution.py:33
  121.7 0.0 reduce-scatter.2.cloned.1.call-update
  121.7 3.1 fusion.3
  124.8 6.4 %convolution_add_fusion = f32[256,2880]{0,1:T(8,128)} fusion(f32[256,2880]{0,1:T(8,128)S(1)} %fusion.3, bf16[256,480]{0,1:T(8,128)(2,1)S(1)} %get-tuple-element.2, bf16[480,8640]{1,0:T(8,128)(2,1)} %bitcast.49), kind=kOutput, calls=%fused_computation.1 | convolution fusion | flops 708526080 | bytes 8970240 | tf_op jit(solution)/shard_map/dot_general | solution.py:25
  131.2 2.3 copy.29
  133.6 82.0 %all_to_all.10 = f32[16,16,2880]{2,1,0:T(8,128)S(1)} all-to-all(f32[16,16,2880]{2,1,0:T(8,128)S(1)} %bitcast.42), channel_id=1, replica_groups=mesh['dp'=2,'expert'=16] {'expert'}, dimensions={0} | all-to-all | bytes 5898240 | tf_op jit(solution)/shard_map/all_to_all | solution.py:44
  215.6 2.2 convolution_convert_fusion.1
  217.8 102.9 %reduce-scatter.2.cloned.1.call-done = f32[240,8640]{1,0:T(8,128)} async-done(((f32[480,8640]{1,0:T(8,128)}), f32[240,8640]{1,0:T(8,128)}) %reduce-scatter.2.cloned.1.call-update) | async-done | bytes 8294416 | tf_op jit(solution)/shard_map/reduce_scatter | solution.py:95
  320.7 0.0 copy-start.1
  320.7 5.8 %convert_bitcast_fusion = bf16[1,240,8640]{2,1,0:T(8,128)(2,1)} fusion(f32[240,8640]{1,0:T(8,128)} %reduce-scatter.2.cloned.1.call-done), kind=kLoop, calls=%fused_computation | loop fusion | flops 2073600 | bytes 12441600 | tf_op jit(solution)/shard_map/broadcast_in_dim | solution.py:104
  326.5 0.0 copy-done.1
  (2 shorter events, 0.0 us)
Async XLA Ops:
  7.2 3.7 %copy-start = (bf16[16,2880]{1,0:T(8,128)(2,1)S(1)}, bf16[16,2880]{1,0:T(8,128)(2,1)}, u32[]{:S(2)}) copy-start(bf16[16,2880]{1,0:T(8,128)(2,1)} %param.8) | copy-start | bytes 276484
  10.0 2.4 copy-start.2
  18.1 7.8 %copy-start.3 = (s32[16]{0:T(128)S(1)}, s32[16]{0:T(128)}, u32[]{:S(2)}) copy-start(s32[16]{0:T(128)} %param.12) | copy-start | bytes 196
  18.1 64.5 %all-to-all-start = ((bf16[16,16,2,2880]{3,1,2,0:T(8,128)(2,1)}), bf16[16,16,2,2880]{3,1,2,0:T(8,128)(2,1)S(1)}, u32[]{:S(2)}, u32[]{:S(2)}) async-start(bf16[16,16,2,2880]{3,1,2,0:T(8,128)(2,1)} %copy.27), calls=%async_computation | async-start | bytes 6029312 | tf_op jit(solution)/shard_map/all_to_all | solution.py:75
  25.7 295.0 %reduce-scatter.2.cloned.1.call-start = ((), (), s32[]{:S(2)}) async-start(), calls=%async_computation.3 | async-start | bytes 25067520 | tf_op jit(solution)/shard_map/reduce_scatter | solution.py:95
  320.7 5.8 %copy-start.1 = (bf16[16,2880]{1,0:T(8,128)(2,1)S(1)}, bf16[16,2880]{1,0:T(8,128)(2,1)}, u32[]{:S(2)}) copy-start(bf16[16,2880]{1,0:T(8,128)(2,1)} %param.8) | copy-start | bytes 276484
Sparse Core Ops, SparseCore 0:
  121.8 198.7 reduce-scatter.1
where the time goes:
time: 334 us; the launch traced here: 333 us
  waiting for transfers between devices  158 us (47%)
  blocking collectives  82 us (25%)
  matrix products  33.1 us (10%)
  local copies, waits for them, and re-layouts  29.9 us (9%)
  between operations  14.2 us (4%)
  other arithmetic  7.99 us (2%)
  starting transfers between devices  7.74 us (2%)
    reduce_scatter x1, waiting for transfers between devices, shards(): lax.psum_scatter(term_block, 'dp', scatter_dimension=0, tiled=True)  103 us
    all_to_all x1, blocking collectives, send_back(): lax.all_to_all(partial_value, 'expert', split_axis=0, concat_axis=0, tile...  82 us
    all_to_all x1, waiting for transfers between devices, shards(): lax.all_to_all(outgoing, 'expert', split_axis=0, concat_axis=0, tiled=True)  55.5 us
    concatenate x1, local copies, waits for them, and re-layouts, weight_terms(): jnp.concatenate([lax.dot_general(grad_gate, token_rows, rows_first, prefe...  19.9 us
    all_to_all x1, starting transfers between devices, shards(): lax.all_to_all(outgoing, 'expert', split_axis=0, concat_axis=0, tiled=True)  7.52 us
  transfers between devices with their start and end apart: 2, of which 2 were waited for; matrix products, arithmetic and copies ran while one was open for 5% of the time, Pallas kernels for 0%

commit v1 on v0

--- a/solution.py
+++ b/solution.py
@@ -2,6 +2,8 @@
 import jax.numpy as jnp
 from jax import lax
 from jax.sharding import PartitionSpec as P
+
+AXES = ("dp", "expert")
 
 
 def silu_parts(preact):
@@ -44,7 +46,7 @@
     return lax.all_to_all(partial_value, "expert", split_axis=0, concat_axis=0, tiled=True)
 
 
-def shards(tokens, grad_out, route_ids, route_prob, device_expert, unit_count, expert_weights):
+def routed_shards(tokens, grad_out, route_ids, route_prob, device_expert, unit_count, expert_weights):
     token_count, width = tokens.shape
     top_count = route_ids.shape[1]
     devices = lax.axis_size("expert")
@@ -104,15 +106,59 @@
     return (grad_tokens.astype(jnp.bfloat16), grad_weights.astype(jnp.bfloat16)[None])
 
 
+def dense_shards(tokens, grad_out, route_ids, route_prob, device_expert, unit_count, expert_weights):
+    width = tokens.shape[1]
+    devices = lax.axis_size("expert")
+    experts = 5 * devices // 16
+    half = expert_weights.shape[1] // lax.axis_size("dp")
+    named = route_ids[:, :, None] == jnp.arange(experts, dtype=jnp.int32)[None, None, :]
+    scales = jnp.sum(jnp.where(named, route_prob[:, :, None], 0.0), axis=1)
+    x = lax.all_gather(tokens, AXES, axis=0, tiled=True)
+    grads = lax.all_gather(grad_out, AXES, axis=0, tiled=True)
+    scales = lax.all_gather(scales, AXES, axis=0, tiled=True)
+    position = lax.axis_index("expert")
+    expert = lax.dynamic_index_in_dim(device_expert, position, keepdims=False)
+    limit = lax.dynamic_index_in_dim(unit_count, position, keepdims=False)
+    scale = jnp.sum(jnp.where(jnp.arange(experts)[None, :] == expert, scales, 0.0), axis=1)
+    dy = (scale[:, None] * grads.astype(jnp.float32)).astype(jnp.bfloat16)
+    first = lax.axis_index("dp") * half
+    weights = lax.dynamic_slice_in_dim(expert_weights[0], first, half, axis=0)
+    mask = (first + jnp.arange(half, dtype=jnp.int32) < limit)[None, :]
+    gate, up, down = (weights[:, i * width : (i + 1) * width] for i in range(3))
+    contract = (((1,), (1,)), ((), ()))
+    rows_first = (((0,), (0,)), ((), ()))
+    f32 = jnp.float32
+    g = lax.dot_general(x, gate, contract, preferred_element_type=f32)
+    v = lax.dot_general(x, up, contract, preferred_element_type=f32)
+    b = lax.dot_general(dy, down, contract, preferred_element_type=f32)
+    sigma = jax.nn.sigmoid(g)
+    active = g * sigma
+    slope = sigma * (1.0 + g * (1.0 - sigma))
+    hidden = jnp.where(mask, active * v, 0.0).astype(jnp.bfloat16)
+    grad_gate = jnp.where(mask, b * v * slope, 0.0).astype(jnp.bfloat16)
+    grad_up = jnp.where(mask, b * active, 0.0).astype(jnp.bfloat16)
+    partial = jnp.dot(grad_gate, gate, preferred_element_type=f32) + jnp.dot(
+        grad_up, up, preferred_element_type=f32
+    )
+    grad_tokens = lax.psum_scatter(partial, AXES, scatter_dimension=0, tiled=True)
+    grad_weights = jnp.concatenate(
+        [
+            lax.dot_general(a, c, rows_first, preferred_element_type=f32).astype(jnp.bfloat16)
+            for a, c in ((grad_gate, x), (grad_up, x), (hidden, dy))
+        ],
+        axis=1,
+    )
+    return grad_tokens.astype(jnp.bfloat16), grad_weights[None]
+
+
+def shards(tokens, grad_out, route_ids, *rest):
+    token_count = tokens.shape[0]
+    capacity = token_count * route_ids.shape[1] * 4 // lax.axis_size("expert")
+    form = dense_shards if capacity >= token_count else routed_shards
+    return form(tokens, grad_out, route_ids, *rest)
+
+
 def solution(mesh):
-    in_specs = (
-        P(("dp", "expert"), None),
-        P(("dp", "expert"), None),
-        P(("dp", "expert"), None),
-        P(("dp", "expert"), None),
-        P(),
-        P(),
-        P("expert", None, None),
-    )
-    out_specs = (P(("dp", "expert"), None), P("expert", "dp", None))
+    in_specs = (P(AXES, None),) * 4 + (P(), P(), P("expert", None, None))
+    out_specs = (P(AXES, None), P("expert", "dp", None))
     return jax.shard_map(shards, mesh=mesh, in_specs=in_specs, out_specs=out_specs, check_vma=False)

time: 334 us -> 295 us (0.88)
  blocking collectives: 82 us -> 43.8 us
  waiting for transfers between devices: 158 us -> 195 us
  local copies, waits for them, and re-layouts: 29.9 us -> 15.1 us
  matrix products: 33.1 us -> 22.4 us
  starting transfers between devices: 7.74 us -> 0.11 us
  other arithmetic: 7.99 us -> 3.68 us
    all_to_all x1 -> x0, blocking collectives: 82 us -> none  [send_back(): lax.all_to_all(partial_value, 'expert', split_axis=0, concat_axis=0, tile...]
    all_gather x0 -> x2, waiting for transfers between devices: none -> 64 us  [the longest x1 53.1 us: dense_shards(): grads = lax.all_gather(grad_out, AXES, axis=0, tiled=True)]
    all_to_all x1 -> x0, waiting for transfers between devices: 55.5 us -> none  [shards(): lax.all_to_all(outgoing, 'expert', split_axis=0, concat_axis=0, tiled=True)]
    all_gather x0 -> x1, blocking collectives: none -> 43.8 us  [dense_shards(): scales = lax.all_gather(scales, AXES, axis=0, tiled=True)]
    reduce_scatter x1, waiting for transfers between devices: 103 us -> 130 us  [dense_shards(): lax.psum_scatter(partial, AXES, scatter_dimension=0, tiled=True)]
    concatenate x1, local copies, waits for them, and re-layouts: 19.9 us -> 7.5 us  [dense_shards(): jnp.concatenate([lax.dot_general(a, c, rows_first, preferred_element_type...]
    dot_general x12 -> x8, matrix products: 33.1 us -> 22.4 us  [the longest x3 6.33 us: dense_shards(): lax.dot_general(a, c, rows_first, preferred_element_type=f32)]
    all_to_all x1 -> x0, starting transfers between devices: 7.52 us -> none  [shards(): lax.all_to_all(outgoing, 'expert', split_axis=0, concat_axis=0, tiled=True)]
  transfers between devices with their start and end apart: 2 -> 3, of which waited for: 2 -> 3; matrix products, arithmetic and copies ran while one was open for 5% -> 10% of each run, Pallas kernels for 0% -> 0%
where the time goes in v1:
time: 295 us; the launch traced here: 294 us
  waiting for transfers between devices  195 us (66%)
  blocking collectives  43.8 us (15%)
  matrix products  22.4 us (8%)
  local copies, waits for them, and re-layouts  15.1 us (5%)
  between operations  13.8 us (5%)
  other arithmetic  3.68 us (1%)
    reduce_scatter x1, waiting for transfers between devices, dense_shards(): lax.psum_scatter(partial, AXES, scatter_dimension=0, tiled=True)  130 us
    all_gather x1, waiting for transfers between devices, dense_shards(): grads = lax.all_gather(grad_out, AXES, axis=0, tiled=True)  53.1 us
    all_gather x1, blocking collectives, dense_shards(): scales = lax.all_gather(scales, AXES, axis=0, tiled=True)  43.8 us
    all_gather x1, waiting for transfers between devices, dense_shards(): x = lax.all_gather(tokens, AXES, axis=0, tiled=True)  10.9 us
    concatenate x1, local copies, waits for them, and re-layouts, dense_shards(): jnp.concatenate([lax.dot_general(a, c, rows_first, preferred_element_type...  7.5 us
    dot_general x3, matrix products, dense_shards(): lax.dot_general(a, c, rows_first, preferred_element_type=f32)  6.33 us
  transfers between devices with their start and end apart: 3, of which 3 were waited for; matrix products, arithmetic and copies ran while one was open for 10% of the time, Pallas kernels for 0%

profile of v1, /device:TPU:0, one launch (start us, length us, event | category | flops | bytes accessed | tf_op | source)
XLA Modules:
  0.0 294.3 jit_solution(11033249698941787515)
XLA Ops:
  7.2 0.0 all-gather.6.cloned.1.call-start
  7.2 0.7 all-gather.6.cloned.1.call-update
  7.9 0.0 all-gather.4.cloned.1.call-start
  7.9 0.7 all-gather.4.cloned.1.call-update
  8.6 0.0 reduce-scatter.2.cloned.1.call-start
  8.7 1.2 dynamic_slice.12
  9.9 1.2 dynamic_slice.13
  11.2 0.7 select_reduce_fusion.1
  11.9 43.8 %all-gather = f32[32,16,5]{1,2,0:T(8,128)S(1)} all-gather(f32[1,16,5]{1,2,0:T(8,128)S(1)} %bitcast.21), channel_id=1, replica_groups=mesh['dp'=2,'expert'=16] {'dp','expert'}, dimensions={0}, use_global_device_ids=true | all-gather | bytes 10560 | tf_op jit(solution)/shard_map/all_gather | solution.py:118
  55.7 0.1 reshape.19
  55.8 0.7 add_compare_fusion
  56.5 0.7 iota_compare_fusion.1
  57.1 0.1 select_reduce_fusion
  57.2 4.5 %dynamic-slice_bitcast_fusion = bf16[240,8640]{1,0:T(8,128)(2,1)} fusion(bf16[1,480,8640]{2,1,0:T(8,128)(2,1)} %param.13, s32[]{:T(128)S(6)} %select_n.29), kind=kLoop, calls=%fused_computation.2 | loop fusion | bytes 8294404 | tf_op jit(solution)/shard_map/dynamic_slice | solution.py:125
  61.7 10.9 %all-gather.6.cloned.1.call-done = bf16[512,2880]{1,0:T(8,128)(2,1)} async-done(((bf16[16,2880]{1,0:T(8,128)(2,1)}), bf16[512,2880]{1,0:T(8,128)(2,1)}) %all-gather.6.cloned.1.call-update) | async-done | bytes 2949136 | tf_op jit(solution)/shard_map/all_gather | solution.py:116
  72.6 0.0 copy-start
  72.6 4.2 %fusion.12 = f32[512,240]{0,1:T(8,128)} fusion(bf16[512,2880]{1,0:T(8,128)(2,1)} %all-gather.6.cloned.1.call-done, bf16[240,8640]{1,0:T(8,128)(2,1)} %dynamic-slice_bitcast_fusion), kind=kOutput, calls=%fused_computation.16 | convolution fusion | flops 707788800 | bytes 4919296 | tf_op jit(solution)/shard_map/dot_general | solution.py:131
  76.8 0.0 copy-done
  76.8 3.2 %fusion.9 = f32[512,240]{0,1:T(8,128)} fusion(bf16[512,2880]{1,0:T(8,128)(2,1)S(1)} %copy-done, bf16[240,8640]{1,0:T(8,128)(2,1)} %dynamic-slice_bitcast_fusion), kind=kOutput, calls=%fused_computation.15 | convolution fusion | flops 707788800 | bytes 4853760 | tf_op jit(solution)/shard_map/dot_general | solution.py:132
  80.0 53.1 %all-gather.4.cloned.1.call-done = bf16[512,2880]{1,0:T(8,128)(2,1)} async-done(((bf16[16,2880]{1,0:T(8,128)(2,1)}), bf16[512,2880]{1,0:T(8,128)(2,1)}) %all-gather.4.cloned.1.call-update) | async-done | bytes 2949136 | tf_op jit(solution)/shard_map/all_gather | solution.py:117
  133.1 0.0 copy-start.1
  133.1 3.9 %select_convert_fusion.1 = (bf16[512,240]{0,1:T(8,128)(2,1)S(1)}, bf16[512,240]{0,1:T(8,128)(2,1)S(1)}) fusion(pred[240]{0:T(512)(128)(4,1)S(1)} %add_compare_fusion, f32[512,240]{0,1:T(8,128)} %fusion.12, f32[512,240]{0,1:T(8,128)} %fusion.9, bf16[240,8640]{1,0:T(8,128)(2,1)} %dynamic-slice_bitcast_fusion, ...), kind=kOutput, calls=%fused_computation.18 | convolution fusion | flops 714055680 | bytes 5904624 | tf_op jit(solution)/shard_map/dot_general | solution.py:133
  137.0 0.0 copy-done.1
  137.0 1.0 fusion.2
  138.0 3.7 %convolution_add_fusion = f32[512,2880]{1,0:T(8,128)} fusion(f32[512,2880]{1,0:T(8,128)S(1)} %fusion.2, bf16[512,240]{0,1:T(8,128)(2,1)S(1)} %get-tuple-element.2, bf16[240,8640]{1,0:T(8,128)(2,1)S(1)} %copy-done.1), kind=kOutput, calls=%fused_computation.1 | convolution fusion | flops 709263360 | bytes 13586432 | tf_op jit(solution)/shard_map/dot_general | solution.py:140
  141.8 0.0 reduce-scatter.2.cloned.1.call-update
  141.8 2.0 convolution_convert_fusion.1
  143.8 0.0 copy-start.4
  143.8 0.0 copy-start.5
  143.8 0.0 copy-start.6
  143.8 2.0 convolution_convert_fusion.2
  145.9 0.0 copy-done.4
  145.9 0.1 copy-done.5
  146.0 0.4 copy-done.6
  146.4 0.0 copy-start.2
  146.4 0.0 copy-start.3
  146.4 2.3 convolution_convert_fusion
  148.7 0.0 copy-done.2
  148.7 0.0 copy-done.3
  148.7 7.5 %concatenate.3 = bf16[240,8640]{1,0:T(8,128)(2,1)} concatenate(bf16[240,2880]{1,0:T(8,128)(2,1)S(1)} %copy-done.3, bf16[240,2880]{1,0:T(8,128)(2,1)S(1)} %copy-done.2, bf16[240,2880]{1,0:T(8,128)(2,1)} %convolution_convert_fusion), dimensions={1} | concatenate | bytes 8294400 | tf_op jit(solution)/shard_map/concatenate | solution.py:144
  156.2 130.0 %reduce-scatter.2.cloned.1.call-done = f32[16,2880]{1,0:T(8,128)} async-done(((f32[512,2880]{1,0:T(8,128)}), f32[16,2880]{1,0:T(8,128)}) %reduce-scatter.2.cloned.1.call-update) | async-done | bytes 184336 | tf_op jit(solution)/shard_map/reduce_scatter | solution.py:143
  286.2 1.6 convert_element_type.31
  (1 shorter events, 0.0 us)
Async XLA Ops:
  7.2 65.4 %all-gather.6.cloned.1.call-start = ((), (), s32[]{:S(2)}) async-start(), calls=%async_computation.2 | async-start | bytes 3108864 | tf_op jit(solution)/shard_map/all_gather | solution.py:116
  7.9 125.2 %all-gather.4.cloned.1.call-start = ((), (), s32[]{:S(2)}) async-start(), calls=%async_computation.1 | async-start | bytes 3108864 | tf_op jit(solution)/shard_map/all_gather | solution.py:117
  8.6 277.5 %reduce-scatter.2.cloned.1.call-start = ((), (), s32[]{:S(2)}) async-start(), calls=%async_computation.3 | async-start | bytes 6217728 | tf_op jit(solution)/shard_map/reduce_scatter | solution.py:143
  72.6 4.2 %copy-start = (bf16[512,2880]{1,0:T(8,128)(2,1)S(1)}, bf16[512,2880]{1,0:T(8,128)(2,1)}, u32[]{:S(2)}) copy-start(bf16[512,2880]{1,0:T(8,128)(2,1)} %all-gather.6.cloned.1.call-done) | copy-start | bytes 8847364
  133.1 3.9 %copy-start.1 = (bf16[240,8640]{1,0:T(8,128)(2,1)S(1)}, bf16[240,8640]{1,0:T(8,128)(2,1)}, u32[]{:S(2)}) copy-start(bf16[240,8640]{1,0:T(8,128)(2,1)} %dynamic-slice_bitcast_fusion) | copy-start | bytes 12441604
  143.8 2.0 copy-start.4
  143.8 2.2 copy-start.5
  143.8 2.6 copy-start.6
  146.4 2.3 copy-start.2
  146.4 2.3 copy-start.3
Sparse Core Ops, SparseCore 0:
  10.8 61.7 all-gather.5
  75.4 57.5 all-gather.3
  141.9 144.2 reduce-scatter.1

commit v2 on v0

--- a/solution.py
+++ b/solution.py
@@ -1,7 +1,13 @@
+import functools
+
 import jax
 import jax.numpy as jnp
 from jax import lax
+from jax.experimental import pallas as pl
+from jax.experimental.pallas import tpu as pltpu
 from jax.sharding import PartitionSpec as P
+
+AXES = ("dp", "expert")
 
 
 def silu_parts(preact):
@@ -44,7 +50,7 @@
     return lax.all_to_all(partial_value, "expert", split_axis=0, concat_axis=0, tiled=True)
 
 
-def shards(tokens, grad_out, route_ids, route_prob, device_expert, unit_count, expert_weights):
+def routed_shards(tokens, grad_out, route_ids, route_prob, device_expert, unit_count, expert_weights):
     token_count, width = tokens.shape
     top_count = route_ids.shape[1]
     devices = lax.axis_size("expert")
@@ -104,15 +110,304 @@
     return (grad_tokens.astype(jnp.bfloat16), grad_weights.astype(jnp.bfloat16)[None])
 
 
+MESH = pl.DeviceIdType.MESH
+STEP = 256
+
+
+def dense_kernel(
+    nz, half, tok, width,
+    x_in, g_in, w_in, sel_ref, mask_ref, gt_out, gw_out,
+    xs, gs, dy, w, wu, gg, gu, hid, acc, send1, recv1, send2a, recv2a, send2b, recv2b,
+    send3a, recv3a, send3b, recv3b, send4, recv4, gw, up,
+    local_sem, recv_sem, sz, sx, sy, ss, rs_send, rs_recv,
+):
+    f32, bf16 = jnp.float32, jnp.bfloat16
+    y = lax.axis_index("dp")
+    position = lax.axis_index("expert")
+    z, x, c = position // 4, (position // 2) % 2, position % 2
+    oy, ox, oc = 1 - y, 1 - x, 1 - c
+
+    def place(yy, zz, xx, cc):
+        return (yy, zz * 4 + xx * 2 + cc)
+
+    def slot(cc, yy, xx, zz):
+        return ((cc * 2 + yy) * 2 + xx) * nz + zz
+
+    def rows(s, count=1):
+        return pl.ds(pl.multiple_of(s * tok, tok), count * tok)
+
+    zs = [lax.rem(z + k, nz) for k in range(nz)]
+    x_nbr, y_nbr, sib = place(y, z, ox, c), place(oy, z, x, c), place(y, z, x, oc)
+    z_nbrs = [place(y, zs[k], x, c) for k in range(1, nz)]
+
+    mine = slot(c, y, x, z)
+    first = pl.multiple_of(y * half, 16)
+    own = [
+        pltpu.make_async_copy(x_in, xs.at[rows(mine)], local_sem.at[0]),
+        pltpu.make_async_copy(g_in, gs.at[rows(mine)], local_sem.at[1]),
+    ]
+    load_w = pltpu.make_async_copy(w_in.at[0, pl.ds(first, half)], w, local_sem.at[2])
+    for copy in own + [load_w]:
+        copy.start()
+    barrier = pltpu.get_barrier_semaphore()
+    peers = [x_nbr, y_nbr, sib] + z_nbrs
+    for peer in peers:
+        pl.semaphore_signal(barrier, inc=1, device_id=peer, device_id_type=MESH)
+    pl.semaphore_wait(barrier, len(peers))
+
+    bufs = (xs, gs)
+    sent = []
+
+    def describe(p, s, target, sem):
+        return pltpu.make_async_remote_copy(
+            src_ref=bufs[p].at[rows(s)], dst_ref=bufs[p].at[rows(s)],
+            send_sem=sem, recv_sem=recv_sem.at[p, s], device_id=target, device_id_type=MESH,
+        )
+
+    counts = {}
+
+    def send(p, s, name, target):
+        sems = {"x": sx, "y": sy, "s": ss, "z": sz}[name]
+        index = counts.get((p, name), 0)
+        counts[(p, name)] = index + 1
+        copy = describe(p, s, target, sems.at[p, index])
+        copy.start()
+        sent.append(copy)
+
+    def arrived(p, s):
+        describe(p, s, sib, ss.at[p, 0]).wait_recv()
+
+    order = [0, 1, nz - 1] + list(range(2, nz - 1))
+    for p in range(2):
+        own[p].wait()
+        for target in z_nbrs:
+            send(p, mine, "z", target)
+        send(p, mine, "x", x_nbr)
+        send(p, mine, "y", y_nbr)
+        send(p, mine, "s", sib)
+    for k in order[1:]:
+        for p in range(2):
+            s = slot(c, y, x, zs[k])
+            arrived(p, s)
+            send(p, s, "x", x_nbr)
+            send(p, s, "y", y_nbr)
+            send(p, s, "s", sib)
+    for k in order:
+        s = slot(c, y, ox, zs[k])
+        arrived(0, s)
+        send(0, s, "y", y_nbr)
+        send(0, s, "s", sib)
+        s = slot(c, oy, x, zs[k])
+        arrived(1, s)
+        send(1, s, "x", x_nbr)
+        send(1, s, "s", sib)
+    load_w.wait()
+    wu[...] = w[:, width : 2 * width]
+    for k in order:
+        for p, s in ((0, slot(c, oy, x, zs[k])), (1, slot(c, y, ox, zs[k]))):
+            arrived(p, s)
+            send(p, s, "s", sib)
+    for k in order:
+        for p in range(2):
+            s = slot(c, oy, ox, zs[k])
+            arrived(p, s)
+            send(p, s, "s", sib)
+    for k in range(nz):
+        for yy in range(2):
+            for xx in range(2):
+                for p in range(2):
+                    arrived(p, slot(oc, yy, xx, k))
+    for copy in sent:
+        copy.wait_send()
+
+    contract = (((1,), (1,)), ((), ()))
+    block = 4 * nz * tok // 2
+    tail = width // 128 * 128
+
+    def forward(i, carry):
+        r = pl.ds(pl.multiple_of(i * block, block), block)
+        scale = jnp.sum(gs[r, tail:].astype(f32) * sel_ref[...], axis=1, keepdims=True)
+        dy[r, :] = (scale * gs[r, :width].astype(f32)).astype(bf16)
+        token_rows = xs[r, :]
+        g = lax.dot_general(token_rows, w[:, :width], contract, preferred_element_type=f32)
+        v = lax.dot_general(token_rows, wu[...], contract, preferred_element_type=f32)
+        b = lax.dot_general(dy[r, :], w[:, 2 * width :], contract, preferred_element_type=f32)
+        live = jnp.broadcast_to(mask_ref[...], g.shape) > 0.0
+        sigma = 1.0 / (1.0 + jnp.exp(-g))
+        active = g * sigma
+        hid[r, :] = jnp.where(live, active * v, 0.0).astype(bf16)
+        gg[r, :] = jnp.where(live, b * v * (sigma * (1.0 + g * (1.0 - sigma))), 0.0).astype(bf16)
+        gu[r, :] = jnp.where(live, b * active, 0.0).astype(bf16)
+        return carry
+
+    lax.fori_loop(0, 8 * nz * tok // block, forward, 0)
+
+    group = nz * tok
+    all_rows = 4 * group
+    cut = (width // 128 + 1) // 2 * 128
+    half_cols = (pl.ds(0, cut), pl.ds(cut, width - cut))
+    spans = [(at, min(STEP, end - at)) for begin, end in ((0, cut), (cut, width)) for at in range(begin, end, STEP)]
+
+    def partial(side, at, size):
+        r = pl.ds(pl.multiple_of(side * all_rows, all_rows), all_rows)
+        return jnp.dot(gg[r, :], w[:, at : at + size], preferred_element_type=f32) + jnp.dot(
+            gu[r, :], wu[:, at : at + size], preferred_element_type=f32
+        )
+
+    def exchange(index, src, dst, target):
+        return pltpu.make_async_remote_copy(
+            src_ref=src, dst_ref=dst, send_sem=rs_send.at[index], recv_sem=rs_recv.at[index],
+            device_id=target, device_id_type=MESH,
+        )
+
+    core = [exchange(h, send1.at[:, half_cols[h]], recv1.at[:, half_cols[h]], sib) for h in range(2)]
+    for at, size in spans:
+        send1[:, at : at + size] = partial(oc, at, size).astype(bf16)
+        if at + size == cut:
+            core[0].start()
+    core[1].start()
+    for at, size in spans:
+        acc[:, at : at + size] = partial(c, at, size)
+
+    def grp(yy, xx, count=1):
+        return pl.ds(pl.multiple_of((yy * 2 + xx) * group, group), count * group)
+
+    lo, hi = slice(0, cut), slice(cut, width)
+    second = [exchange(2, send2a, recv2a, y_nbr), exchange(3, send2b, recv2b, x_nbr)]
+    core[0].wait()
+    r = grp(oy, 0, 2)
+    send2a[...] = (acc[r, lo] + recv1[r, lo].astype(f32)).astype(bf16)
+    second[0].start()
+    core[1].wait()
+    for yy in range(2):
+        r = grp(yy, ox)
+        send2b[yy * group : (yy + 1) * group, :] = (acc[r, hi] + recv1[r, hi].astype(f32)).astype(bf16)
+    second[1].start()
+    r = grp(y, 0, 2)
+    acc[r, lo] = acc[r, lo] + recv1[r, lo].astype(f32)
+    for yy in range(2):
+        r = grp(yy, x)
+        acc[r, hi] = acc[r, hi] + recv1[r, hi].astype(f32)
+
+    def weight_term(left, right, store):
+        turned = left[...].T
+        for at in range(0, width, STEP):
+            size = min(STEP, width - at)
+            store(at, size, jnp.dot(turned, right[:, at : at + size], preferred_element_type=f32).astype(bf16))
+
+    def store_at(base):
+        def store(at, size, value):
+            gw[:, base + at : base + at + size] = value
+        return store
+
+    weight_term(gg, xs, store_at(0))
+
+    third = [exchange(4, send3a, recv3a, x_nbr), exchange(5, send3b, recv3b, y_nbr)]
+    part = lambda i: pl.ds(pl.multiple_of(i * group, group), group)
+    second[0].wait()
+    send3a[...] = (acc[grp(y, ox), lo] + recv2a[part(ox), :].astype(f32)).astype(bf16)
+    third[0].start()
+    second[1].wait()
+    send3b[...] = (acc[grp(oy, x), hi] + recv2b[part(oy), :].astype(f32)).astype(bf16)
+    third[1].start()
+    r = grp(y, x)
+    acc[r, lo] = acc[r, lo] + recv2a[part(x), :].astype(f32)
+    acc[r, hi] = acc[r, hi] + recv2b[part(y), :].astype(f32)
+
+    weight_term(gu, xs, store_at(width))
+
+    third[0].wait()
+    third[1].wait()
+    acc[r, lo] = acc[r, lo] + recv3a[...].astype(f32)
+    acc[r, hi] = acc[r, hi] + recv3b[...].astype(f32)
+    send4[...] = acc[r, :].astype(bf16)
+    last = []
+    for k in range(1, nz):
+        last.append(exchange(5 + k, send4.at[rows(zs[k])], recv4.at[pl.ds((k - 1) * tok, tok)], z_nbrs[k - 1]))
+        last[-1].start()
+
+    weight_term(hid, dy, store_at(2 * width))
+    store_w = pltpu.make_async_copy(gw, gw_out.at[0], local_sem.at[3])
+    store_w.start()
+
+    total = acc[pl.ds(pl.multiple_of((y * 2 + x) * group + z * tok, tok), tok), :]
+    for k in range(1, nz):
+        last[k - 1].wait()
+        total = total + recv4[(k - 1) * tok : k * tok, :].astype(f32)
+    gt_out[...] = total.astype(bf16)
+    store_w.wait()
+
+
+def dense_shards(tokens, grad_out, route_ids, route_prob, device_expert, unit_count, expert_weights):
+    tok, width = tokens.shape
+    devices = lax.axis_size("expert")
+    nz = devices // 4
+    experts = 5 * devices // 16
+    half = expert_weights.shape[1] // lax.axis_size("dp")
+    named = route_ids[:, :, None] == jnp.arange(experts, dtype=jnp.int32)[None, None, :]
+    scales = jnp.sum(jnp.where(named, route_prob[:, :, None], 0.0), axis=1)
+    high = lax.reduce_precision(scales, 8, 7)
+    middle = lax.reduce_precision(scales - high, 8, 7)
+    spare = 128 - width % 128
+    terms = jnp.concatenate([high, middle, scales - high - middle], axis=1).astype(jnp.bfloat16)
+    assert 3 * experts <= spare
+    terms = jnp.pad(terms, ((0, 0), (0, spare - 3 * experts)))
+    padded = width + spare
+    grads = jnp.concatenate([grad_out, terms], axis=1)
+    position = lax.axis_index("expert")
+    expert = lax.dynamic_index_in_dim(device_expert, position, keepdims=False)
+    limit = lax.dynamic_index_in_dim(unit_count, position, keepdims=False)
+    lane = jnp.arange(128, dtype=jnp.int32) - width % 128
+    sel = ((lane >= 0) & (lane < 3 * experts) & (lane % experts == expert)).astype(jnp.float32)[None]
+    first = lax.axis_index("dp") * half
+    mask = (first + jnp.arange(half, dtype=jnp.int32) < limit).astype(jnp.float32)[None]
+    n = 2 * devices * tok
+    group = nz * tok
+    cut = (width // 128 + 1) // 2 * 128
+    rest = width - cut
+    bf16, f32 = jnp.bfloat16, jnp.float32
+    vmem = pltpu.VMEM
+    dma = pltpu.SemaphoreType.DMA
+    any_spec = pl.BlockSpec(memory_space=pl.ANY)
+    vmem_spec = pl.BlockSpec(memory_space=pltpu.VMEM)
+    return pl.pallas_call(
+        functools.partial(dense_kernel, nz, half, tok, width),
+        out_shape=(
+            jax.ShapeDtypeStruct((tok, width), bf16),
+            jax.ShapeDtypeStruct((1, half, 3 * width), bf16),
+        ),
+        in_specs=[any_spec, any_spec, any_spec, vmem_spec, vmem_spec],
+        out_specs=(vmem_spec, any_spec),
+        scratch_shapes=[
+            vmem((n, width), bf16), vmem((n, padded), bf16), vmem((n, width), bf16),
+            vmem((half, 3 * width), bf16), vmem((half, width), bf16),
+            vmem((n, half), bf16), vmem((n, half), bf16), vmem((n, half), bf16),
+            vmem((4 * group, width), f32),
+            vmem((4 * group, width), bf16), vmem((4 * group, width), bf16),
+            vmem((2 * group, cut), bf16), vmem((2 * group, cut), bf16),
+            vmem((2 * group, rest), bf16), vmem((2 * group, rest), bf16),
+            vmem((group, cut), bf16), vmem((group, cut), bf16),
+            vmem((group, rest), bf16), vmem((group, rest), bf16),
+            vmem((group, width), bf16), vmem(((nz - 1) * tok, width), bf16),
+            vmem((half, 3 * width), bf16), vmem((16, 128), bf16),
+            dma((4,)), dma((2, 2 * devices)), dma((2, nz)), dma((2, 2 * nz)), dma((2, 2 * nz)),
+            dma((2, 4 * nz)), dma((5 + nz,)), dma((5 + nz,)),
+        ],
+        compiler_params=pltpu.CompilerParams(
+            collective_id=0, has_side_effects=True, vmem_limit_bytes=60 * 1024 * 1024
+        ),
+        name="dense_backward",
+    )(tokens, grads, expert_weights, sel, mask)
+
+
+def shards(tokens, grad_out, route_ids, *rest):
+    token_count = tokens.shape[0]
+    capacity = token_count * route_ids.shape[1] * 4 // lax.axis_size("expert")
+    form = dense_shards if capacity >= token_count else routed_shards
+    return form(tokens, grad_out, route_ids, *rest)
+
+
 def solution(mesh):
-    in_specs = (
-        P(("dp", "expert"), None),
-        P(("dp", "expert"), None),
-        P(("dp", "expert"), None),
-        P(("dp", "expert"), None),
-        P(),
-        P(),
-        P("expert", None, None),
-    )
-    out_specs = (P(("dp", "expert"), None), P("expert", "dp", None))
+    in_specs = (P(AXES, None),) * 4 + (P(), P(), P("expert", None, None))
+    out_specs = (P(AXES, None), P("expert", "dp", None))
     return jax.shard_map(shards, mesh=mesh, in_specs=in_specs, out_specs=out_specs, check_vma=False)

time: 334 us -> 91 us (0.27)
  waiting for transfers between devices: 158 us -> 0 us
  blocking collectives: 82 us -> 0 us
  Pallas kernels: 0 us -> 76.5 us
  matrix products: 33.1 us -> 0 us
  local copies, waits for them, and re-layouts: 29.9 us -> 8.64 us
  between operations: 14.2 us -> 0.66 us
  starting transfers between devices: 7.74 us -> 0 us
    reduce_scatter x1 -> x0, waiting for transfers between devices: 103 us -> none  [shards(): lax.psum_scatter(term_block, 'dp', scatter_dimension=0, tiled=True)]
    all_to_all x1 -> x0, blocking collectives: 82 us -> none  [send_back(): lax.all_to_all(partial_value, 'expert', split_axis=0, concat_axis=0, tile...]
    pallas_call x0 -> x1, Pallas kernels: none -> 76.5 us  [dense_shards(): pl.pallas_call(functools.partial(dense_kernel, nz, half, tok, width), out...]
    all_to_all x1 -> x0, waiting for transfers between devices: 55.5 us -> none  [shards(): lax.all_to_all(outgoing, 'expert', split_axis=0, concat_axis=0, tiled=True)]
    dot_general x12 -> x0, matrix products: 33.1 us -> none  [the longest x1 6.42 us: unit_work(): jnp.dot(grad_up, up_rows, preferred_element_type=jnp.float32)]
    concatenate x1 -> x0, local copies, waits for them, and re-layouts: 19.9 us -> none  [weight_terms(): jnp.concatenate([lax.dot_general(grad_gate, token_rows, rows_first, prefe...]
    all_to_all x1 -> x0, starting transfers between devices: 7.52 us -> none  [shards(): lax.all_to_all(outgoing, 'expert', split_axis=0, concat_axis=0, tiled=True)]
    broadcast_in_dim x1 -> x0, other arithmetic: 5.82 us -> none  [shards(): grad_weights.astype(jnp.bfloat16)[None]]
  transfers between devices with their start and end apart: 2 -> 0, of which waited for: 2 -> 0; matrix products, arithmetic and copies ran while one was open for 5% -> 0% of each run, Pallas kernels for 0% -> 0%
where the time goes in v2:
time: 91 us; the launch traced here: 90.7 us
  Pallas kernels  76.5 us (84%)
  local copies, waits for them, and re-layouts  8.64 us (9%)
  other arithmetic  4.86 us (5%)
    pallas_call x1, Pallas kernels, dense_shards(): pl.pallas_call(functools.partial(dense_kernel, nz, half, tok, width), out...  76.5 us
    unnamed x2, local copies, waits for them, and re-layouts  5.99 us

profile of v2, /device:TPU:0, one launch (start us, length us, event | category | flops | bytes accessed | tf_op | source)
XLA Modules:
  0.0 90.7 jit_solution(13941617819410563090)
XLA Ops:
  0.6 1.2 %dynamic_slice.8 = s32[1]{0:T(128)} dynamic-slice(s32[16]{0:T(128)} %param.12, s32[]{:T(128)S(6)} %select_n.25), dynamic_slice_sizes={1} | dynamic-slice | bytes 12 | tf_op jit(solution)/shard_map/jit(dynamic_index_in_dim)/dynamic_slice | solution.py:359
  1.9 1.2 %compare_convert_fusion.mask_ref = f32[1,240]{1,0:T(1,128)} fusion(s32[]{:T(128)} %bitcast.1, s32[]{:T(128)S(6)} %mul.3), kind=kLoop, calls=%fused_computation.12 | loop fusion | flops 720 | bytes 968 | tf_op jit(solution)/shard_map/convert_element_type | solution.py:363
  3.1 1.2 %dynamic_slice.7 = s32[1]{0:T(128)} dynamic-slice(s32[16]{0:T(128)} %param.11, s32[]{:T(128)S(6)} %select_n.25), dynamic_slice_sizes={1} | dynamic-slice | bytes 12 | tf_op jit(solution)/shard_map/jit(dynamic_index_in_dim)/dynamic_slice | solution.py:358
  4.3 1.2 %and_convert_fusion.sel_ref = f32[1,128]{1,0:T(1,128)} fusion(s32[]{:T(128)} %bitcast), kind=kLoop, calls=%fused_computation.13 | loop fusion | flops 1664 | bytes 516 | tf_op jit(solution)/shard_map/convert_element_type | solution.py:361
  5.6 0.7 select_reduce_fusion
  6.3 0.1 copy.14
  6.4 0.1 copy.13
  6.5 0.1 fusion.5
  6.5 1.6 %pad_maximum_fusion.g_in = bf16[16,2944]{1,0:T(8,128)(2,1)} fusion(bf16[16,64]{1,0:T(8,128)(2,1)S(1)} %fusion.5, bf16[16,2880]{1,0:T(8,128)(2,1)} %param.8), kind=kLoop, calls=%fused_computation | loop fusion | flops 188416 | bytes 188416 | tf_op jit(solution)/shard_map/concatenate | solution.py:356
  8.2 76.5 %dense_backward.1 = (bf16[16,2880]{1,0:T(8,128)(2,1)}, bf16[1,240,8640]{2,1,0:T(8,128)(2,1)}) custom-call(bf16[16,2880]{1,0:T(8,128)(2,1)} %x_in.1, bf16[16,2944]{1,0:T(8,128)(2,1)} %pad_maximum_fusion.g_in, bf16[1,480,8640]{2,1,0:T(8,128)(2,1)} %w_in.1, f32[1,128]{1,0:T(1,128)} %and_convert_fusion.sel_ref, f32[1,240]{1,0:T(1,128)} %compare_convert_fusion.mask_ref), custom_call_target="tpu_custom_call" | custom-call | tf_op jit(solution)/shard_map/dense_backward/pallas_call | solution.py:373
  84.7 1.5 %copy.18 = bf16[16,2880]{1,0:T(8,128)(2,1)} copy(bf16[16,2880]{1,0:T(8,128)(2,1)} %get-tuple-element.7) | data formatting | bytes 184320
  86.2 4.5 %copy.19 = bf16[1,240,8640]{2,1,0:T(8,128)(2,1)} copy(bf16[1,240,8640]{2,1,0:T(8,128)(2,1)} %get-tuple-element.8) | data formatting | bytes 8294400
  (2 shorter events, 0.0 us)

commit v3 on v2

--- a/solution.py
+++ b/solution.py
@@ -115,8 +115,8 @@
 
 
 def dense_kernel(
-    nz, half, tok, width,
-    x_in, g_in, w_in, sel_ref, mask_ref, gt_out, gw_out,
+    nz, half, tok, width, experts,
+    x_in, g_in, w_in, ids_ref, prob_ref, expert_ref, limit_ref, gt_out, gw_out,
     xs, gs, dy, w, wu, gg, gu, hid, acc, send1, recv1, send2a, recv2a, send2b, recv2b,
     send3a, recv3a, send3b, recv3b, send4, recv4, gw, up,
     local_sem, recv_sem, sz, sx, sy, ss, rs_send, rs_recv,
@@ -139,24 +139,35 @@
     zs = [lax.rem(z + k, nz) for k in range(nz)]
     x_nbr, y_nbr, sib = place(y, z, ox, c), place(oy, z, x, c), place(y, z, x, oc)
     z_nbrs = [place(y, zs[k], x, c) for k in range(1, nz)]
+    z_sides = (place(y, lax.rem(z + nz - 1, nz), x, c), place(y, lax.rem(z + 1, nz), x, c))
+    has_side = (z > 0, z < nz - 1)
 
     mine = slot(c, y, x, z)
     first = pl.multiple_of(y * half, 16)
-    own = [
-        pltpu.make_async_copy(x_in, xs.at[rows(mine)], local_sem.at[0]),
-        pltpu.make_async_copy(g_in, gs.at[rows(mine)], local_sem.at[1]),
-    ]
+    own_x = pltpu.make_async_copy(x_in, xs.at[rows(mine)], local_sem.at[0])
     load_w = pltpu.make_async_copy(w_in.at[0, pl.ds(first, half)], w, local_sem.at[2])
-    for copy in own + [load_w]:
+    for copy in (own_x, load_w):
         copy.start()
     barrier = pltpu.get_barrier_semaphore()
     peers = [x_nbr, y_nbr, sib] + z_nbrs
     for peer in peers:
         pl.semaphore_signal(barrier, inc=1, device_id=peer, device_id_type=MESH)
+
+    spare = gs.shape[1] - width
+    lane = lax.broadcasted_iota(jnp.int32, (tok, spare), 1)
+    scales = jnp.zeros((tok, spare), f32)
+    for k in range(ids_ref.shape[1]):
+        scales += jnp.where(ids_ref[:, k : k + 1] == lane % experts, prob_ref[:, k : k + 1], 0.0)
+    high = scales.astype(bf16).astype(f32)
+    middle = (scales - high).astype(bf16).astype(f32)
+    term = lane // experts
+    packed = jnp.where(term == 0, high, jnp.where(term == 1, middle, scales - high - middle))
+    gs[rows(mine), :width] = g_in[...]
+    gs[rows(mine), width:] = jnp.where(term < 3, packed, 0.0).astype(bf16)
+    own_x.wait()
     pl.semaphore_wait(barrier, len(peers))
 
     bufs = (xs, gs)
-    sent = []
 
     def describe(p, s, target, sem):
         return pltpu.make_async_remote_copy(
@@ -164,75 +175,109 @@
             send_sem=sem, recv_sem=recv_sem.at[p, s], device_id=target, device_id_type=MESH,
         )
 
-    counts = {}
-
-    def send(p, s, name, target):
-        sems = {"x": sx, "y": sy, "s": ss, "z": sz}[name]
-        index = counts.get((p, name), 0)
-        counts[(p, name)] = index + 1
-        copy = describe(p, s, target, sems.at[p, index])
-        copy.start()
-        sent.append(copy)
-
     def arrived(p, s):
         describe(p, s, sib, ss.at[p, 0]).wait_recv()
 
-    order = [0, 1, nz - 1] + list(range(2, nz - 1))
+    def along_z(p, zz, side):
+        return describe(p, slot(c, y, x, zz), z_sides[side], sz.at[p, side, zz])
+
+    def to_x(p, yy, zz):
+        return describe(p, slot(c, yy, x, zz), x_nbr, sx.at[p, (yy if p else 0) * nz + zz])
+
+    def to_y(p, xx, zz):
+        return describe(p, slot(c, y, xx, zz), y_nbr, sy.at[p, (0 if p else xx) * nz + zz])
+
+    def to_sib(p, yy, xx, zz):
+        return describe(p, slot(c, yy, xx, zz), sib, ss.at[p, (yy * 2 + xx) * nz + zz])
+
+    def spread(p, zz):
+        to_x(p, y, zz).start()
+        to_y(p, x, zz).start()
+        to_sib(p, y, x, zz).start()
+
+    def relay(zz):
+        arrived(0, slot(c, y, ox, zz))
+        to_y(0, ox, zz).start()
+        to_sib(0, y, ox, zz).start()
+        arrived(1, slot(c, oy, x, zz))
+        to_x(1, oy, zz).start()
+        to_sib(1, oy, x, zz).start()
+
+    def at_distance(d, act):
+        for side, zz in ((0, z - d), (1, z + d)):
+            pl.when((zz >= 0) & (zz < nz))(functools.partial(act, side, zz))
+
+    def from_z(side, zz):
+        for p in range(2):
+            arrived(p, slot(c, y, x, zz))
+            pl.when(has_side[1 - side])(lambda: along_z(p, zz, 1 - side).start())
+            spread(p, zz)
+
     for p in range(2):
-        own[p].wait()
-        for target in z_nbrs:
-            send(p, mine, "z", target)
-        send(p, mine, "x", x_nbr)
-        send(p, mine, "y", y_nbr)
-        send(p, mine, "s", sib)
-    for k in order[1:]:
-        for p in range(2):
-            s = slot(c, y, x, zs[k])
-            arrived(p, s)
-            send(p, s, "x", x_nbr)
-            send(p, s, "y", y_nbr)
-            send(p, s, "s", sib)
-    for k in order:
-        s = slot(c, y, ox, zs[k])
-        arrived(0, s)
-        send(0, s, "y", y_nbr)
-        send(0, s, "s", sib)
-        s = slot(c, oy, x, zs[k])
-        arrived(1, s)
-        send(1, s, "x", x_nbr)
-        send(1, s, "s", sib)
+        for side in range(2):
+            pl.when(has_side[side])(lambda: along_z(p, z, side).start())
+        spread(p, z)
+    for d in range(1, nz):
+        at_distance(d, from_z)
+        if d == 1:
+            relay(z)
+        else:
+            at_distance(d - 1, lambda side, zz: relay(zz))
+    at_distance(nz - 1, lambda side, zz: relay(zz))
     load_w.wait()
     wu[...] = w[:, width : 2 * width]
-    for k in order:
-        for p, s in ((0, slot(c, oy, x, zs[k])), (1, slot(c, y, ox, zs[k]))):
-            arrived(p, s)
-            send(p, s, "s", sib)
-    for k in order:
-        for p in range(2):
-            s = slot(c, oy, ox, zs[k])
-            arrived(p, s)
-            send(p, s, "s", sib)
+
+    def finish(zz):
+        for p, yy, xx in ((0, oy, x), (1, y, ox), (0, oy, ox), (1, oy, ox)):
+            arrived(p, slot(c, yy, xx, zz))
+            to_sib(p, yy, xx, zz).start()
+
+    finish(z)
+    for d in range(1, nz):
+        at_distance(d, lambda side, zz: finish(zz))
     for k in range(nz):
         for yy in range(2):
             for xx in range(2):
                 for p in range(2):
                     arrived(p, slot(oc, yy, xx, k))
-    for copy in sent:
-        copy.wait_send()
-
+
+    def drain_z(side, zz):
+        for p in range(2):
+            pl.when(has_side[1 - side])(lambda: along_z(p, zz, 1 - side).wait_send())
+
+    for p in range(2):
+        for side in range(2):
+            pl.when(has_side[side])(lambda: along_z(p, z, side).wait_send())
+    for d in range(1, nz):
+        at_distance(d, drain_z)
+    for k in range(nz):
+        for p in range(2):
+            to_x(p, y, k).wait_send()
+            to_y(p, x, k).wait_send()
+            for yy in range(2):
+                for xx in range(2):
+                    to_sib(p, yy, xx, k).wait_send()
+        to_y(0, ox, k).wait_send()
+        to_x(1, oy, k).wait_send()
+
+    expert = expert_ref[position]
+    lane = lax.broadcasted_iota(jnp.int32, (1, 128), 1) - (128 - spare)
+    sel = jnp.where((lane >= 0) & (lane < 3 * experts) & (lane % experts == expert), 1.0, 0.0)
+    unit = lax.broadcasted_iota(jnp.int32, (1, half), 1) + y * half
+    unit_mask = jnp.where(unit < limit_ref[position], 1.0, 0.0)
     contract = (((1,), (1,)), ((), ()))
     block = 4 * nz * tok // 2
     tail = width // 128 * 128
 
     def forward(i, carry):
         r = pl.ds(pl.multiple_of(i * block, block), block)
-        scale = jnp.sum(gs[r, tail:].astype(f32) * sel_ref[...], axis=1, keepdims=True)
+        scale = jnp.sum(gs[r, tail:].astype(f32) * sel, axis=1, keepdims=True)
         dy[r, :] = (scale * gs[r, :width].astype(f32)).astype(bf16)
         token_rows = xs[r, :]
         g = lax.dot_general(token_rows, w[:, :width], contract, preferred_element_type=f32)
         v = lax.dot_general(token_rows, wu[...], contract, preferred_element_type=f32)
         b = lax.dot_general(dy[r, :], w[:, 2 * width :], contract, preferred_element_type=f32)
-        live = jnp.broadcast_to(mask_ref[...], g.shape) > 0.0
+        live = jnp.broadcast_to(unit_mask, g.shape) > 0.0
         sigma = 1.0 / (1.0 + jnp.exp(-g))
         active = g * sigma
         hid[r, :] = jnp.where(live, active * v, 0.0).astype(bf16)
@@ -344,23 +389,9 @@
     nz = devices // 4
     experts = 5 * devices // 16
     half = expert_weights.shape[1] // lax.axis_size("dp")
-    named = route_ids[:, :, None] == jnp.arange(experts, dtype=jnp.int32)[None, None, :]
-    scales = jnp.sum(jnp.where(named, route_prob[:, :, None], 0.0), axis=1)
-    high = lax.reduce_precision(scales, 8, 7)
-    middle = lax.reduce_precision(scales - high, 8, 7)
     spare = 128 - width % 128
-    terms = jnp.concatenate([high, middle, scales - high - middle], axis=1).astype(jnp.bfloat16)
     assert 3 * experts <= spare
-    terms = jnp.pad(terms, ((0, 0), (0, spare - 3 * experts)))
     padded = width + spare
-    grads = jnp.concatenate([grad_out, terms], axis=1)
-    position = lax.axis_index("expert")
-    expert = lax.dynamic_index_in_dim(device_expert, position, keepdims=False)
-    limit = lax.dynamic_index_in_dim(unit_count, position, keepdims=False)
-    lane = jnp.arange(128, dtype=jnp.int32) - width % 128
-    sel = ((lane >= 0) & (lane < 3 * experts) & (lane % experts == expert)).astype(jnp.float32)[None]
-    first = lax.axis_index("dp") * half
-    mask = (first + jnp.arange(half, dtype=jnp.int32) < limit).astype(jnp.float32)[None]
     n = 2 * devices * tok
     group = nz * tok
     cut = (width // 128 + 1) // 2 * 128
@@ -369,14 +400,15 @@
     vmem = pltpu.VMEM
     dma = pltpu.SemaphoreType.DMA
     any_spec = pl.BlockSpec(memory_space=pl.ANY)
+    smem_spec = pl.BlockSpec(memory_space=pltpu.SMEM)
     vmem_spec = pl.BlockSpec(memory_space=pltpu.VMEM)
     return pl.pallas_call(
-        functools.partial(dense_kernel, nz, half, tok, width),
+        functools.partial(dense_kernel, nz, half, tok, width, experts),
         out_shape=(
             jax.ShapeDtypeStruct((tok, width), bf16),
             jax.ShapeDtypeStruct((1, half, 3 * width), bf16),
         ),
-        in_specs=[any_spec, any_spec, any_spec, vmem_spec, vmem_spec],
+        in_specs=[any_spec, vmem_spec, any_spec, vmem_spec, vmem_spec, smem_spec, smem_spec],
         out_specs=(vmem_spec, any_spec),
         scratch_shapes=[
             vmem((n, width), bf16), vmem((n, padded), bf16), vmem((n, width), bf16),
@@ -390,14 +422,14 @@
             vmem((group, rest), bf16), vmem((group, rest), bf16),
             vmem((group, width), bf16), vmem(((nz - 1) * tok, width), bf16),
             vmem((half, 3 * width), bf16), vmem((16, 128), bf16),
-            dma((4,)), dma((2, 2 * devices)), dma((2, nz)), dma((2, 2 * nz)), dma((2, 2 * nz)),
+            dma((4,)), dma((2, 2 * devices)), dma((2, 2, nz)), dma((2, 2 * nz)), dma((2, 2 * nz)),
             dma((2, 4 * nz)), dma((5 + nz,)), dma((5 + nz,)),
         ],
         compiler_params=pltpu.CompilerParams(
             collective_id=0, has_side_effects=True, vmem_limit_bytes=60 * 1024 * 1024
         ),
         name="dense_backward",
-    )(tokens, grads, expert_weights, sel, mask)
+    )(tokens, grad_out, expert_weights, route_ids, route_prob, device_expert, unit_count)
 
 
 def shards(tokens, grad_out, route_ids, *rest):

time: 91 us -> 79.2 us (0.87)
  Pallas kernels: 76.5 us -> 69.6 us
  other arithmetic: 4.86 us -> 0 us
    pallas_call x1, Pallas kernels: 76.5 us -> 69.6 us  [dense_shards(): pl.pallas_call(functools.partial(dense_kernel, nz, half, tok, width, expe...]
    unnamed x2 -> x4, local copies, waits for them, and re-layouts: 5.99 us -> 8.7 us
    dynamic_slice x2 -> x0, local copies, waits for them, and re-layouts: 2.48 us -> none  [the longest x1 1.24 us: dense_shards(): limit = lax.dynamic_index_in_dim(unit_count, position, keepdims=False)]
    convert_element_type x2 -> x0, other arithmetic: 2.45 us -> none  [the longest x1 1.24 us: dense_shards(): ((lane >= 0) & (lane < 3 * experts) & (lane % experts == expert)).astype(...]
    concatenate x2 -> x0, other arithmetic: 1.69 us -> none  [the longest x1 1.61 us: dense_shards(): grads = jnp.concatenate([grad_out, terms], axis=1)]
where the time goes in v3:
time: 79.2 us; the launch traced here: 79 us
  Pallas kernels  69.6 us (88%)
  local copies, waits for them, and re-layouts  8.7 us (11%)
    pallas_call x1, Pallas kernels, dense_shards(): pl.pallas_call(functools.partial(dense_kernel, nz, half, tok, width, expe...  69.6 us
    unnamed x4, local copies, waits for them, and re-layouts  8.7 us

profile of v3, /device:TPU:0, one launch (start us, length us, event | category | flops | bytes accessed | tf_op | source)
XLA Modules:
  0.0 79.0 jit_solution(1096478270575295363)
XLA Ops:
  0.6 1.4 %copy.9.ids_ref = s32[16,4]{1,0:T(8,128)} copy(s32[16,4]{0,1:T(4,128)} %param.9) | data formatting | bytes 512 | tf_op args[2]
  2.0 1.4 %copy.10.prob_ref = f32[16,4]{1,0:T(8,128)} copy(f32[16,4]{0,1:T(4,128)} %param.10) | data formatting | bytes 512 | tf_op args[3]
  3.3 69.6 %dense_backward.1 = (bf16[16,2880]{1,0:T(8,128)(2,1)}, bf16[1,240,8640]{2,1,0:T(8,128)(2,1)}) custom-call(bf16[16,2880]{1,0:T(8,128)(2,1)} %x_in.1, bf16[16,2880]{1,0:T(8,128)(2,1)} %g_in.1, bf16[1,480,8640]{2,1,0:T(8,128)(2,1)} %w_in.1, s32[16,4]{1,0:T(8,128)} %copy.9.ids_ref, f32[16,4]{1,0:T(8,128)} %copy.10.prob_ref, s32[16]{0:T(128)} %expert_ref.1, ...), custom_call_target="tpu_custom_call" | custom-call | tf_op jit(solution)/shard_map/dense_backward/pallas_call | solution.py:405
  73.0 1.5 %copy.13 = bf16[16,2880]{1,0:T(8,128)(2,1)} copy(bf16[16,2880]{1,0:T(8,128)(2,1)} %get-tuple-element.4) | data formatting | bytes 184320
  74.5 4.5 %copy.14 = bf16[1,240,8640]{2,1,0:T(8,128)(2,1)} copy(bf16[1,240,8640]{2,1,0:T(8,128)(2,1)} %get-tuple-element.5) | data formatting | bytes 8294400

commit v4 on v3

--- a/solution.py
+++ b/solution.py
@@ -117,8 +117,8 @@
 def dense_kernel(
     nz, half, tok, width, experts,
     x_in, g_in, w_in, ids_ref, prob_ref, expert_ref, limit_ref, gt_out, gw_out,
-    xs, gs, dy, w, wu, gg, gu, hid, acc, send1, recv1, send2a, recv2a, send2b, recv2b,
-    send3a, recv3a, send3b, recv3b, send4, recv4, gw, up,
+    xs, gs, dy, w, wu, gate_pre, up_pre, gg, gu, hid, acc, send1, recv1, send2, recv2,
+    send3, recv3, send4, recv4, gw,
     local_sem, recv_sem, sz, sx, sy, ss, rs_send, rs_recv,
 ):
     f32, bf16 = jnp.float32, jnp.bfloat16
@@ -224,8 +224,39 @@
         else:
             at_distance(d - 1, lambda side, zz: relay(zz))
     at_distance(nz - 1, lambda side, zz: relay(zz))
+    expert = expert_ref[position]
+    lane = lax.broadcasted_iota(jnp.int32, (1, 128), 1) - (128 - spare)
+    sel = jnp.where((lane >= 0) & (lane < 3 * experts) & (lane % experts == expert), 1.0, 0.0)
+    unit = lax.broadcasted_iota(jnp.int32, (1, half), 1) + y * half
+    unit_mask = jnp.where(unit < limit_ref[position], 1.0, 0.0)
+    contract = (((1,), (1,)), ((), ()))
+    block = 2 * nz * tok
+    tail = width // 128 * 128
+
+    def block_rows(cc, yy):
+        return pl.ds(pl.multiple_of((cc * 2 + yy) * block, block), block)
+
+    def gate_up(cc, yy):
+        r = block_rows(cc, yy)
+        gate_pre[r, :] = lax.dot_general(xs[r, :], w[:, :width], contract, preferred_element_type=f32)
+        up_pre[r, :] = lax.dot_general(xs[r, :], wu[...], contract, preferred_element_type=f32)
+
+    def backward(cc, yy):
+        r = block_rows(cc, yy)
+        scale = jnp.sum(gs[r, tail:].astype(f32) * sel, axis=1, keepdims=True)
+        dy[r, :] = (scale * gs[r, :width].astype(f32)).astype(bf16)
+        b = lax.dot_general(dy[r, :], w[:, 2 * width :], contract, preferred_element_type=f32)
+        g, v = gate_pre[r, :], up_pre[r, :]
+        live = jnp.broadcast_to(unit_mask, g.shape) > 0.0
+        sigma = 1.0 / (1.0 + jnp.exp(-g))
+        active = g * sigma
+        hid[r, :] = jnp.where(live, active * v, 0.0).astype(bf16)
+        gg[r, :] = jnp.where(live, b * v * (sigma * (1.0 + g * (1.0 - sigma))), 0.0).astype(bf16)
+        gu[r, :] = jnp.where(live, b * active, 0.0).astype(bf16)
+
     load_w.wait()
     wu[...] = w[:, width : 2 * width]
+    gate_up(c, y)
 
     def finish(zz):
         for p, yy, xx in ((0, oy, x), (1, y, ox), (0, oy, ox), (1, oy, ox)):
@@ -233,13 +264,126 @@
             to_sib(p, yy, xx, zz).start()
 
     finish(z)
-    for d in range(1, nz):
+    for d in range(1, nz - 1):
         at_distance(d, lambda side, zz: finish(zz))
     for k in range(nz):
-        for yy in range(2):
-            for xx in range(2):
-                for p in range(2):
-                    arrived(p, slot(oc, yy, xx, k))
+        for xx in range(2):
+            arrived(0, slot(oc, y, xx, k))
+    gate_up(oc, y)
+    at_distance(nz - 1, lambda side, zz: finish(zz))
+    gate_up(c, oy)
+    backward(c, y)
+    backward(c, oy)
+    for k in range(nz):
+        for xx in range(2):
+            arrived(0, slot(oc, oy, xx, k))
+            arrived(1, slot(oc, y, xx, k))
+            arrived(1, slot(oc, oy, xx, k))
+    gate_up(oc, oy)
+    backward(oc, y)
+    backward(oc, oy)
+
+    group = nz * tok
+    all_rows = 4 * group
+    quarter = (width // 128 + 4) // 4 * 128
+    strips = [(at, min(at + quarter, width)) for at in range(0, width, quarter)]
+    count = len(strips)
+
+    def spans(begin, end):
+        return [(at, min(STEP, end - at)) for at in range(begin, end, STEP)]
+
+    def partial(side, at, size):
+        r = pl.ds(pl.multiple_of(side * all_rows, all_rows), all_rows)
+        return jnp.dot(gg[r, :], w[:, at : at + size], preferred_element_type=f32) + jnp.dot(
+            gu[r, :], wu[:, at : at + size], preferred_element_type=f32
+        )
+
+    def exchange(index, src, dst, target):
+        return pltpu.make_async_remote_copy(
+            src_ref=src, dst_ref=dst, send_sem=rs_send.at[index], recv_sem=rs_recv.at[index],
+            device_id=target, device_id_type=MESH,
+        )
+
+    def grp(yy, xx):
+        return pl.ds(pl.multiple_of((yy * 2 + xx) * group, group), group)
+
+    def part(i):
+        return pl.ds(pl.multiple_of(i * group, group), group)
+
+    def strip_ref(ref, i):
+        begin, end = strips[i]
+        return ref.at[:, pl.ds(begin, end - begin)]
+
+    core, second, third, last = [], [], [], []
+    for i in range(count):
+        even = i % 2 == 0
+        core.append(exchange(i, strip_ref(send1, i), strip_ref(recv1, i), sib))
+        second.append(exchange(count + i, strip_ref(send2, i), strip_ref(recv2, i), y_nbr if even else x_nbr))
+        third.append(exchange(2 * count + i, strip_ref(send3, i), strip_ref(recv3, i), x_nbr if even else y_nbr))
+
+    for i, (begin, end) in enumerate(strips):
+        for at, size in spans(begin, end):
+            send1[:, at : at + size] = partial(oc, at, size).astype(bf16)
+        core[i].start()
+
+    def second_stage(i):
+        begin, end = strips[i]
+        cols = slice(begin, end)
+        for at, size in spans(begin, end):
+            acc[:, at : at + size] = partial(c, at, size)
+        core[i].wait()
+        for j in range(2):
+            r = grp(oy, j) if i % 2 == 0 else grp(j, ox)
+            send2[j * group : (j + 1) * group, cols] = (acc[r, cols] + recv1[r, cols].astype(f32)).astype(bf16)
+        second[i].start()
+        for j in range(2):
+            r = grp(y, j) if i % 2 == 0 else grp(j, x)
+            acc[r, cols] = acc[r, cols] + recv1[r, cols].astype(f32)
+
+    def third_stage(i):
+        cols = slice(*strips[i])
+        away, stay, r = (ox, x, grp(y, ox)) if i % 2 == 0 else (oy, y, grp(oy, x))
+        second[i].wait()
+        send3[:, cols] = (acc[r, cols] + recv2[part(away), cols].astype(f32)).astype(bf16)
+        third[i].start()
+        r = grp(y, x)
+        acc[r, cols] = acc[r, cols] + recv2[part(stay), cols].astype(f32)
+
+    def last_stage(i):
+        begin, end = strips[i]
+        cols = slice(begin, end)
+        r = grp(y, x)
+        third[i].wait()
+        acc[r, cols] = acc[r, cols] + recv3[:, cols].astype(f32)
+        send4[:, cols] = acc[r, cols].astype(bf16)
+        for k in range(1, nz):
+            copy = exchange(
+                3 * count + i * (nz - 1) + k - 1,
+                send4.at[rows(zs[k]), pl.ds(begin, end - begin)],
+                recv4.at[pl.ds((k - 1) * tok, tok), pl.ds(begin, end - begin)],
+                z_nbrs[k - 1],
+            )
+            copy.start()
+            last.append(copy)
+
+    def weight_term(left, right, base):
+        turned = left[...].T
+        for at, size in spans(0, width):
+            value = jnp.dot(turned, right[:, at : at + size], preferred_element_type=f32)
+            gw[:, base + at : base + at + size] = value.astype(bf16)
+
+    for i in range(count):
+        second_stage(i)
+    weight_term(gg, xs, 0)
+    for i in range(count):
+        third_stage(i)
+        if i == 1:
+            weight_term(gu, xs, width)
+    for i in range(count):
+        last_stage(i)
+    weight_term(hid, dy, 2 * width)
+    store_w = pltpu.make_async_copy(gw, gw_out.at[0], local_sem.at[3])
+    store_w.start()
 
     def drain_z(side, zz):
         for p in range(2):
@@ -260,124 +404,10 @@
         to_y(0, ox, k).wait_send()
         to_x(1, oy, k).wait_send()
 
-    expert = expert_ref[position]
-    lane = lax.broadcasted_iota(jnp.int32, (1, 128), 1) - (128 - spare)
-    sel = jnp.where((lane >= 0) & (lane < 3 * experts) & (lane % experts == expert), 1.0, 0.0)
-    unit = lax.broadcasted_iota(jnp.int32, (1, half), 1) + y * half
-    unit_mask = jnp.where(unit < limit_ref[position], 1.0, 0.0)
-    contract = (((1,), (1,)), ((), ()))
-    block = 4 * nz * tok // 2
-    tail = width // 128 * 128
-
-    def forward(i, carry):
-        r = pl.ds(pl.multiple_of(i * block, block), block)
-        scale = jnp.sum(gs[r, tail:].astype(f32) * sel, axis=1, keepdims=True)
-        dy[r, :] = (scale * gs[r, :width].astype(f32)).astype(bf16)
-        token_rows = xs[r, :]
-        g = lax.dot_general(token_rows, w[:, :width], contract, preferred_element_type=f32)
-        v = lax.dot_general(token_rows, wu[...], contract, preferred_element_type=f32)
-        b = lax.dot_general(dy[r, :], w[:, 2 * width :], contract, preferred_element_type=f32)
-        live = jnp.broadcast_to(unit_mask, g.shape) > 0.0
-        sigma = 1.0 / (1.0 + jnp.exp(-g))
-        active = g * sigma
-        hid[r, :] = jnp.where(live, active * v, 0.0).astype(bf16)
-        gg[r, :] = jnp.where(live, b * v * (sigma * (1.0 + g * (1.0 - sigma))), 0.0).astype(bf16)
-        gu[r, :] = jnp.where(live, b * active, 0.0).astype(bf16)
-        return carry
-
-    lax.fori_loop(0, 8 * nz * tok // block, forward, 0)
-
-    group = nz * tok
-    all_rows = 4 * group
-    cut = (width // 128 + 1) // 2 * 128
-    half_cols = (pl.ds(0, cut), pl.ds(cut, width - cut))
-    spans = [(at, min(STEP, end - at)) for begin, end in ((0, cut), (cut, width)) for at in range(begin, end, STEP)]
-
-    def partial(side, at, size):
-        r = pl.ds(pl.multiple_of(side * all_rows, all_rows), all_rows)
-        return jnp.dot(gg[r, :], w[:, at : at + size], preferred_element_type=f32) + jnp.dot(
-            gu[r, :], wu[:, at : at + size], preferred_element_type=f32
-        )
-
-    def exchange(index, src, dst, target):
-        return pltpu.make_async_remote_copy(
-            src_ref=src, dst_ref=dst, send_sem=rs_send.at[index], recv_sem=rs_recv.at[index],
-            device_id=target, device_id_type=MESH,
-        )
-
-    core = [exchange(h, send1.at[:, half_cols[h]], recv1.at[:, half_cols[h]], sib) for h in range(2)]
-    for at, size in spans:
-        send1[:, at : at + size] = partial(oc, at, size).astype(bf16)
-        if at + size == cut:
-            core[0].start()
-    core[1].start()
-    for at, size in spans:
-        acc[:, at : at + size] = partial(c, at, size)
-
-    def grp(yy, xx, count=1):
-        return pl.ds(pl.multiple_of((yy * 2 + xx) * group, group), count * group)
-
-    lo, hi = slice(0, cut), slice(cut, width)
-    second = [exchange(2, send2a, recv2a, y_nbr), exchange(3, send2b, recv2b, x_nbr)]
-    core[0].wait()
-    r = grp(oy, 0, 2)
-    send2a[...] = (acc[r, lo] + recv1[r, lo].astype(f32)).astype(bf16)
-    second[0].start()
-    core[1].wait()
-    for yy in range(2):
-        r = grp(yy, ox)
-        send2b[yy * group : (yy + 1) * group, :] = (acc[r, hi] + recv1[r, hi].astype(f32)).astype(bf16)
-    second[1].start()
-    r = grp(y, 0, 2)
-    acc[r, lo] = acc[r, lo] + recv1[r, lo].astype(f32)
-    for yy in range(2):
-        r = grp(yy, x)
-        acc[r, hi] = acc[r, hi] + recv1[r, hi].astype(f32)
-
-    def weight_term(left, right, store):
-        turned = left[...].T
-        for at in range(0, width, STEP):
-            size = min(STEP, width - at)
-            store(at, size, jnp.dot(turned, right[:, at : at + size], preferred_element_type=f32).astype(bf16))
-
-    def store_at(base):
-        def store(at, size, value):
-            gw[:, base + at : base + at + size] = value
-        return store
-
-    weight_term(gg, xs, store_at(0))
-
-    third = [exchange(4, send3a, recv3a, x_nbr), exchange(5, send3b, recv3b, y_nbr)]
-    part = lambda i: pl.ds(pl.multiple_of(i * group, group), group)
-    second[0].wait()
-    send3a[...] = (acc[grp(y, ox), lo] + recv2a[part(ox), :].astype(f32)).astype(bf16)
-    third[0].start()
-    second[1].wait()
-    send3b[...] = (acc[grp(oy, x), hi] + recv2b[part(oy), :].astype(f32)).astype(bf16)
-    third[1].start()
-    r = grp(y, x)
-    acc[r, lo] = acc[r, lo] + recv2a[part(x), :].astype(f32)
-    acc[r, hi] = acc[r, hi] + recv2b[part(y), :].astype(f32)
-
-    weight_term(gu, xs, store_at(width))
-
-    third[0].wait()
-    third[1].wait()
-    acc[r, lo] = acc[r, lo] + recv3a[...].astype(f32)
-    acc[r, hi] = acc[r, hi] + recv3b[...].astype(f32)
-    send4[...] = acc[r, :].astype(bf16)
-    last = []
+    total = acc[pl.ds(pl.multiple_of((y * 2 + x) * group + z * tok, tok), tok), :]
+    for copy in last:
+        copy.wait()
     for k in range(1, nz):
-        last.append(exchange(5 + k, send4.at[rows(zs[k])], recv4.at[pl.ds((k - 1) * tok, tok)], z_nbrs[k - 1]))
-        last[-1].start()
-
-    weight_term(hid, dy, store_at(2 * width))
-    store_w = pltpu.make_async_copy(gw, gw_out.at[0], local_sem.at[3])
-    store_w.start()
-
-    total = acc[pl.ds(pl.multiple_of((y * 2 + x) * group + z * tok, tok), tok), :]
-    for k in range(1, nz):
-        last[k - 1].wait()
         total = total + recv4[(k - 1) * tok : k * tok, :].astype(f32)
     gt_out[...] = total.astype(bf16)
     store_w.wait()
@@ -394,8 +424,6 @@
     padded = width + spare
     n = 2 * devices * tok
     group = nz * tok
-    cut = (width // 128 + 1) // 2 * 128
-    rest = width - cut
     bf16, f32 = jnp.bfloat16, jnp.float32
     vmem = pltpu.VMEM
     dma = pltpu.SemaphoreType.DMA
@@ -413,17 +441,16 @@
         scratch_shapes=[
             vmem((n, width), bf16), vmem((n, padded), bf16), vmem((n, width), bf16),
             vmem((half, 3 * width), bf16), vmem((half, width), bf16),
+            vmem((n, half), f32), vmem((n, half), f32),
             vmem((n, half), bf16), vmem((n, half), bf16), vmem((n, half), bf16),
             vmem((4 * group, width), f32),
             vmem((4 * group, width), bf16), vmem((4 * group, width), bf16),
-            vmem((2 * group, cut), bf16), vmem((2 * group, cut), bf16),
-            vmem((2 * group, rest), bf16), vmem((2 * group, rest), bf16),
-            vmem((group, cut), bf16), vmem((group, cut), bf16),
-            vmem((group, rest), bf16), vmem((group, rest), bf16),
+            vmem((2 * group, width), bf16), vmem((2 * group, width), bf16),
+            vmem((group, width), bf16), vmem((group, width), bf16),
             vmem((group, width), bf16), vmem(((nz - 1) * tok, width), bf16),
-            vmem((half, 3 * width), bf16), vmem((16, 128), bf16),
+            vmem((half, 3 * width), bf16),
             dma((4,)), dma((2, 2 * devices)), dma((2, 2, nz)), dma((2, 2 * nz)), dma((2, 2 * nz)),
-            dma((2, 4 * nz)), dma((5 + nz,)), dma((5 + nz,)),
+            dma((2, 4 * nz)), dma((4 * (nz + 2),)), dma((4 * (nz + 2),)),
         ],
         compiler_params=pltpu.CompilerParams(
             collective_id=0, has_side_effects=True, vmem_limit_bytes=60 * 1024 * 1024

time: 79.2 us -> 73.8 us (0.932)
  Pallas kernels: 69.6 us -> 64.2 us
    pallas_call x1, Pallas kernels: 69.6 us -> 64.2 us  [dense_shards(): pl.pallas_call(functools.partial(dense_kernel, nz, half, tok, width, expe...]
where the time goes in v4:
time: 73.8 us; the launch traced here: 73.6 us
  Pallas kernels  64.2 us (87%)
  local copies, waits for them, and re-layouts  8.7 us (12%)
    pallas_call x1, Pallas kernels, dense_shards(): pl.pallas_call(functools.partial(dense_kernel, nz, half, tok, width, expe...  64.2 us
    unnamed x4, local copies, waits for them, and re-layouts  8.7 us

profile of v4, /device:TPU:0, one launch (start us, length us, event | category | flops | bytes accessed | tf_op | source)
XLA Modules:
  0.0 73.6 jit_solution(17043879499203916226)
XLA Ops:
  0.6 1.4 %copy.9.ids_ref = s32[16,4]{1,0:T(8,128)} copy(s32[16,4]{0,1:T(4,128)} %param.9) | data formatting | bytes 512 | tf_op args[2]
  2.0 1.4 %copy.10.prob_ref = f32[16,4]{1,0:T(8,128)} copy(f32[16,4]{0,1:T(4,128)} %param.10) | data formatting | bytes 512 | tf_op args[3]
  3.3 64.2 %dense_backward.1 = (bf16[16,2880]{1,0:T(8,128)(2,1)}, bf16[1,240,8640]{2,1,0:T(8,128)(2,1)}) custom-call(bf16[16,2880]{1,0:T(8,128)(2,1)} %x_in.1, bf16[16,2880]{1,0:T(8,128)(2,1)} %g_in.1, bf16[1,480,8640]{2,1,0:T(8,128)(2,1)} %w_in.1, s32[16,4]{1,0:T(8,128)} %copy.9.ids_ref, f32[16,4]{1,0:T(8,128)} %copy.10.prob_ref, s32[16]{0:T(128)} %expert_ref.1, ...), custom_call_target="tpu_custom_call" | custom-call | tf_op jit(solution)/shard_map/dense_backward/pallas_call | solution.py:433
  67.6 1.5 %copy.13 = bf16[16,2880]{1,0:T(8,128)(2,1)} copy(bf16[16,2880]{1,0:T(8,128)(2,1)} %get-tuple-element.4) | data formatting | bytes 184320
  69.1 4.5 %copy.14 = bf16[1,240,8640]{2,1,0:T(8,128)(2,1)} copy(bf16[1,240,8640]{2,1,0:T(8,128)(2,1)} %get-tuple-element.5) | data formatting | bytes 8294400
